TPU v7x, 32 devices: a whole 2x2x4 slice. The times are simulated.
32 devices in a mesh: expert: 16 (over z, y, x), tensor: 2 (over core).
Axes of the slice: x: 2, y: 2, z: 4, core: 2. Of those that a mesh axis runs over, the one named last changes fastest.
Arguments:
- moe_in: bfloat16 [4096, 1536], P('expert', 'tensor'), may hold values from -6 to 6
- moe_grad: bfloat16 [4096, 1536], P('expert', 'tensor'), may hold values from -6 to 6
- routes: int32 [4096, 2], P('expert'), may hold values from 0 to 15, all different within a row; in each aligned block of 256 rows (0 to 255, 256 to 511, ...) at most 64 rows name the same one
- gates: float32 [4096, 2], P('expert'), may hold values from 0.25 to 1
- w_in: bfloat16 [16, 1536, 3072], P('expert', None, 'tensor'), may hold values from -0.15625 to 0.15625
- w_out: bfloat16 [16, 3072, 1536], P('expert', 'tensor'), may hold values from -0.109375 to 0.109375
- conv_in: bfloat16 [4096, 1536], P('expert', 'tensor'), may hold values from -6 to 6
- w_glu: bfloat16 [1536, 2, 1536], P(None, None, 'tensor'), may hold values from -0.15625 to 0.15625
- kernel: float32 [32, 1536], P(None, 'tensor'), may hold values from -1 to 1
- conv_grad: bfloat16 [4096, 1536], P('expert', 'tensor'), may hold values from -6 to 6
Outputs:
- moe_input_grad: bfloat16 [1536, 4096], P('tensor', 'expert')
- conv_input_grad: bfloat16 [1536, 4096], P('tensor', 'expert')
Inputs may be any that keep to these rules, and one draw needn't show every extreme that they name: `routes`: each row names two different experts. Among the 256 frames of one index of the expert axis no expert is named by more than 64 of them, a bound that some block reaches.
All inputs are finite; a program needn't handle non-finite values.
Results may differ from a plain program's by a relative error of at most 0.0072.
Values may be sent and summed in bfloat16 or wider, within the bound.
No kernel may reach another device: no remote copies, remote signals or barrier semaphores. Data moves between devices by JAX's collectives and lax.ppermute only.
A program may use at most 128 MiB of HBM per device.

v0:
```python
import jax
import jax.numpy as jnp
from jax import lax
from jax.sharding import PartitionSpec as P


def from_behind(x, axis, by):
    devices = lax.axis_size(axis)
    pairs = [(i, i + by) for i in range(devices) if 0 <= i + by < devices]
    return lax.ppermute(x, axis, pairs)


def body(moe_in, moe_grad, routes, gates, w_in, w_out, conv_in, w_glu, kernel, conv_grad):
    frames = moe_in.shape[0]
    channels = conv_grad.shape[1]
    local = w_in.shape[0]
    sources = lax.axis_size("expert")
    experts = local * sources
    capacity = 4 * frames // experts
    slots = experts * capacity
    pairs = 2 * frames
    model = w_in.shape[1]
    glu_weight = w_glu.reshape(model, 2 * channels)
    flat = routes.reshape(pairs)
    onehot = (flat[:, None] == jnp.arange(experts, dtype=jnp.int32)[None, :]).astype(jnp.int32)
    position = jnp.sum(onehot * jnp.cumsum(onehot, axis=0), axis=1) - 1
    slot = flat * capacity + position
    source = jnp.full((slots,), pairs, jnp.int32).at[slot].set(jnp.arange(pairs, dtype=jnp.int32))
    scaled = (moe_grad.astype(jnp.float32)[:, None, :] * gates[:, :, None]).astype(jnp.bfloat16)
    scaled = jnp.concatenate(
        [scaled.reshape(pairs, channels), jnp.zeros((1, channels), jnp.bfloat16)], axis=0
    )
    padded_in = jnp.concatenate([moe_in, jnp.zeros((1, channels), jnp.bfloat16)], axis=0)
    x_send = padded_in[source // 2]
    g_send = scaled[source]
    x_recv, g_recv = (
        lax.all_to_all(x_send, "expert", split_axis=0, concat_axis=0, tiled=True),
        lax.all_to_all(g_send, "expert", split_axis=0, concat_axis=0, tiled=True),
    )
    pieces = (
        lax.all_gather(x_recv, "tensor", axis=1, tiled=True),
        lax.all_gather(g_recv, "tensor", axis=1, tiled=True),
    )
    width = pieces[0].shape[1]
    x_part = pieces[0].reshape(sources, local, capacity, width)
    g_part = pieces[1].reshape(sources, local, capacity, width)
    first = jnp.einsum("sqcd,qdh->sqch", x_part, w_in, preferred_element_type=jnp.float32)
    second = jnp.einsum("sqcd,qhd->sqch", g_part, w_out, preferred_element_type=jnp.float32)
    rows_glu = glu_weight
    glu_pre = jnp.dot(
        lax.all_gather(conv_in, "tensor", axis=1, tiled=True),
        rows_glu,
        preferred_element_type=jnp.float32,
    )
    sig = jax.nn.sigmoid(first)
    pre_grad = (second * sig * (1.0 + first * (1.0 - sig))).astype(jnp.bfloat16)
    term = jnp.einsum("qih,sqch->isqc", w_in, pre_grad, preferred_element_type=jnp.float32)
    slot_grads = lax.psum_scatter(
        term.reshape(channels * lax.axis_size("tensor"), slots).astype(jnp.bfloat16),
        "tensor",
        scatter_dimension=0,
        tiled=True,
    )
    returned = lax.all_to_all(slot_grads, "expert", split_axis=1, concat_axis=1, tiled=True)
    picked = returned[:, slot].astype(jnp.float32).reshape(channels, frames, 2)
    moe_input_grad = jnp.sum(picked, axis=2).astype(jnp.bfloat16)
    taps = kernel.shape[0]
    future = from_behind(conv_grad[: taps - 1], "expert", -1)
    extended = jnp.concatenate([conv_grad, future], axis=0).astype(jnp.float32)
    mix_grad = jnp.zeros((frames, channels), jnp.float32)
    for offset in range(taps):
        mix_grad = mix_grad + kernel[offset] * extended[offset : offset + frames]
    value = glu_pre[:, :channels]
    gate = glu_pre[:, channels:]
    sig_gate = jax.nn.sigmoid(gate)
    glu_grad = jnp.concatenate(
        [mix_grad * sig_gate, mix_grad * value * sig_gate * (1.0 - sig_gate)], axis=1
    ).astype(jnp.bfloat16)
    rows_glu = glu_weight
    conv_input_grad = lax.psum_scatter(
        lax.dot_general(
            rows_glu, glu_grad, (((1,), (1,)), ((), ())), preferred_element_type=jnp.float32
        ).astype(jnp.bfloat16),
        "tensor",
        scatter_dimension=0,
        tiled=True,
    )
    return (moe_input_grad, conv_input_grad)


def solution(mesh):
    placed = (
        P("expert", "tensor"),
        P("expert", "tensor"),
        P("expert", None),
        P("expert", None),
        P("expert", None, "tensor"),
        P("expert", "tensor", None),
        P("expert", "tensor"),
        P(None, None, "tensor"),
        P(None, "tensor"),
        P("expert", "tensor"),
    )
    return jax.shard_map(
        body,
        mesh=mesh,
        in_specs=placed,
        out_specs=(P("tensor", "expert"), P("tensor", "expert")),
        check_vma=False,
    )
```

profile of v0, /device:TPU:12, one launch (start us, length us, event | category | flops | bytes accessed | tf_op | source)
XLA Modules:
  0.0 207.2 jit_solution(6990360619382237161)
XLA Ops:
  7.2 0.7 broadcast_multiply_fusion
  7.8 0.8 copy.21
  8.7 0.1 eq.25
  8.8 0.1 eq.29
  9.0 0.1 copy.20
  9.1 0.1 mul.385
  9.3 1.2 reduce-window.6
  10.4 0.2 slice_reduce_fusion
  10.7 0.1 fusion.62
  10.8 2.4 %scatter_custom_fusion = s32[1024]{0:T(1024)S(1)} fusion(s32[512]{0:T(512)S(1)} %bitcast.104, s32[512]{0:T(512)S(1)} %iota.11, s32[]{:T(128)} %constant.14.clone.1), kind=kCustom, calls=%fused_computation.153 | custom fusion | bytes 4100 | tf_op jit(solution)/shard_map/scatter | solution.py:28
  13.3 1.0 concatenate.14
  14.3 5.2 %gather_fusion.1 = bf16[1024,768]{1,0:T(8,128)(2,1)} fusion(bf16[257,768]{1,0:T(8,128)(2,1)S(1)} %concatenate.14, s32[1024]{0:T(1024)S(1)} %get-tuple-element.43), kind=kCustom, calls=%fused_computation.1 | custom fusion | bytes 3149824 | tf_op jit(solution)/shard_map/gather | solution.py:34
  19.5 7.3 %all-to-all-start.1 = ((bf16[16,64,768]{2,1,0:T(8,128)(2,1)}), bf16[16,64,768]{2,1,0:T(8,128)(2,1)S(1)}, u32[]{:S(2)}, u32[]{:S(2)}) async-start(bf16[16,64,768]{2,1,0:T(8,128)(2,1)} %bitcast.11), calls=%async_computation.1 | async-start | bytes 3145728 | tf_op jit(solution)/shard_map/all_to_all | solution.py:37
  26.9 1.6 mul.378
  28.4 2.4 %mul.379 = f32[512,768]{1,0:T(8,128)S(1)} reshape(f32[256,2,768]{2,1,0:T(2,128)} %mul.378) | data formatting | bytes 3145728 | tf_op jit(solution)/shard_map/mul | solution.py:29
  30.8 0.1 copy.19
  31.0 0.1 mul.380
  31.1 32.9 %all-to-all-done.1 = bf16[16,64,768]{2,1,0:T(8,128)(2,1)S(1)} async-done(((bf16[16,64,768]{2,1,0:T(8,128)(2,1)}), bf16[16,64,768]{2,1,0:T(8,128)(2,1)S(1)}, u32[]{:S(2)}, u32[]{:S(2)}) %all-to-all-start.1) | async-done | bytes 1572896 | tf_op jit(solution)/shard_map/all_to_all | solution.py:37
  64.0 1.2 copy-done
  65.2 0.0 all-gather.3.cloned.1.call-start
  65.2 0.1 multiply_convert_fusion
  65.4 0.1 concatenate.13
  65.4 4.0 %gather_fusion = bf16[1024,768]{1,0:T(8,128)(2,1)S(1)} fusion(bf16[513,768]{1,0:T(8,128)(2,1)S(1)} %concatenate.13, s32[1024]{0:T(1024)S(1)} %get-tuple-element.42), kind=kCustom, calls=%fused_computation | custom fusion | bytes 3149824 | tf_op jit(solution)/shard_map/gather | solution.py:35
  69.4 40.3 %all_to_all.36 = bf16[16,64,768]{2,1,0:T(8,128)(2,1)} all-to-all(bf16[16,64,768]{2,1,0:T(8,128)(2,1)S(1)} %bitcast.97), channel_id=1, replica_groups=mesh['expert'=16,'tensor'=2] {'expert'}, dimensions={0} | all-to-all | bytes 3145728 | tf_op jit(solution)/shard_map/all_to_all | solution.py:38
  109.7 0.0 reduce-scatter.3.cloned.1.call-start
  109.8 9.8 %fusion.8 = f32[16,64,1536]{2,1,0:T(8,128)} fusion(bf16[16,64,1536]{2,1,0:T(8,128)(2,1)} %bitcast.109, bf16[1,1536,1536]{2,1,0:T(8,128)(2,1)} %param.14), kind=kOutput, calls=%fused_computation.15 | convolution fusion | flops 4831838208 | bytes 14155776 | tf_op jit(solution)/shard_map/sqcd,qdh->sqch/dot_general | solution.py:47
  119.6 1.8 all-gather.3.cloned.1.call-done
  121.4 10.2 %fusion.17 = bf16[16,64,1536]{2,1,0:T(8,128)(2,1)S(1)} fusion(f32[16,64,1536]{2,1,0:T(8,128)} %fusion.8, bf16[16,64,1536]{2,1,0:T(8,128)(2,1)} %bitcast.110, bf16[1,1536,1536]{2,1,0:T(8,128)(2,1)} %param.15), kind=kOutput, calls=%fused_computation.20 | convolution fusion | flops 4845993984 | bytes 17301504 | tf_op jit(solution)/shard_map/sqcd,qhd->sqch/dot_general | solution.py:48
  131.6 6.5 %fusion.14 = bf16[16,64,1536]{2,1,0:T(8,128)(2,1)} fusion(bf16[16,64,1536]{2,1,0:T(8,128)(2,1)S(1)} %fusion.17, bf16[1,1536,1536]{2,1,0:T(8,128)(2,1)S(1)} %bitcast.108), kind=kOutput, calls=%fused_computation.19 | convolution fusion | flops 4833411072 | bytes 11010048 | tf_op jit(solution)/shard_map/qih,sqch->isqc/dot_general | solution.py:57
  138.1 1.0 copy-done.3
  139.1 3.4 %collective-permute-start = (bf16[31,768]{1,0:T(8,128)(2,1)S(1)}, bf16[31,768]{1,0:T(8,128)(2,1)S(1)}, u32[]{:S(2)}, u32[]{:S(2)}) collective-permute-start(bf16[31,768]{1,0:T(8,128)(2,1)S(1)} %slice.210), channel_id=1, source_target_pairs={{2,0},{4,2},{6,4},{8,6},{10,8},{12,10},{14,12},{16,14},{18,16},{20... | collective-permute-start | bytes 142856 | tf_op jit(solution)/shard_map/ppermute | solution.py:10
  142.5 3.3 %copy.27 = bf16[192,8,2,768]{3,1,2,0:T(8,128)(2,1)S(1)} copy(bf16[192,8,2,768]{3,2,1,0:T(2,128)(2,1)} %bitcast.98) | data formatting | bytes 9437184
  145.8 0.2 slice_reduce_fusion.32
  146.0 2.5 %all_gather.11 = bf16[256,1536]{1,0:T(8,128)(2,1)S(1)} all-gather(bf16[256,768]{1,0:T(8,128)(2,1)S(1)} %copy-done.4), channel_id=1, replica_groups=mesh['expert'=16,'tensor'=2] {'tensor'}, dimensions={1}, use_global_device_ids=true | all-gather | bytes 1179648 | tf_op jit(solution)/shard_map/all_gather | solution.py:51
  148.5 2.6 %fusion.72 = f32[256,1536]{1,0:T(8,128)} fusion(bf16[256,1536]{1,0:T(8,128)(2,1)S(1)} %all_gather.11, bf16[1536,1536]{1,0:T(8,128)(2,1)S(1)} %bitcast.99), kind=kOutput, calls=%fused_computation.158 | convolution fusion | flops 1207959552 | bytes 7077888 | tf_op jit(solution)/shard_map/dot_general | solution.py:50
  151.1 0.1 slice_reduce_fusion.31
  151.2 0.1 maximum_convert_fusion
  151.3 6.6 %all-to-all-start.2 = ((bf16[768,16,64]{0,2,1:T(8,128)(2,1)}), bf16[768,16,64]{0,2,1:T(8,128)(2,1)S(1)}, u32[]{:S(2)}, u32[]{:S(2)}) async-start(bf16[768,16,64]{0,2,1:T(8,128)(2,1)} %bitcast.103), calls=%async_computation.3 | async-start | bytes 3145728 | tf_op jit(solution)/shard_map/all_to_all | solution.py:64
  158.0 4.4 %multiply_convert_fusion.1 = (bf16[256,768]{1,0:T(8,128)(2,1)S(1)}, f32[256,768]{1,0:T(8,128)S(1)}) fusion(f32[256,1536]{1,0:T(8,128)} %fusion.72, f32[287,768]{1,0:T(8,128)S(1)} %maximum_convert_fusion, f32[768]{0:T(1024)S(1)} %get-tuple-element.38, f32[768]{0:T(1024)S(1)} %get-tuple-element.39, f32[768]{0:T(1024)S(1)} %get-tuple-element.9, ...), kind=kLoop, calls=%fused_computation.98 | loop fusion | flops 13369344 | bytes 27230208 | tf_op jit(solution)/shard_map/convert.1
  162.5 0.2 fusion.23
  162.7 4.6 %fusion.20 = bf16[1536,256]{0,1:T(8,128)(2,1)} fusion(bf16[1536,1536]{1,0:T(8,128)(2,1)} %bitcast.100, bf16[256,768]{1,0:T(8,128)(2,1)S(1)} %fusion.23, bf16[256,768]{1,0:T(8,128)(2,1)S(1)} %get-tuple-element.40), kind=kOutput, calls=%fused_computation.22 | convolution fusion | flops 1209925632 | bytes 6291456 | tf_op jit(solution)/shard_map/dot_general | solution.py:81
  167.4 9.4 %reduce-scatter.5.cloned.1.call-done = bf16[768,256]{0,1:T(8,128)(2,1)} async-done(((bf16[1536,256]{0,1:T(8,128)(2,1)}), bf16[768,256]{0,1:T(8,128)(2,1)}) %reduce-scatter.5.cloned.1.call-update) | async-done | bytes 393232 | tf_op jit(solution)/shard_map/reduce_scatter | solution.py:80
  176.8 1.9 copy.25
  178.7 16.6 %all-to-all-done.2 = bf16[768,16,64]{0,2,1:T(8,128)(2,1)S(1)} async-done(((bf16[768,16,64]{0,2,1:T(8,128)(2,1)}), bf16[768,16,64]{0,2,1:T(8,128)(2,1)S(1)}, u32[]{:S(2)}, u32[]{:S(2)}) %all-to-all-start.2) | async-done | bytes 1572896 | tf_op jit(solution)/shard_map/all_to_all | solution.py:64
  195.3 2.0 gather_fusion.2
  197.3 0.3 gather.14
  197.6 2.1 %reduce_sum.22 = bf16[768,256]{0,1:T(8,128)(2,1)S(1)} reduce(bf16[768,256,2]{0,2,1:T(2,128)(2,1)S(1)} %gather.14, bf16[]{:T(256)} %constant.13.clone.1), dimensions={2}, to_apply=%region_5.6 | reduce | flops 196608 | bytes 1179650 | tf_op jit(solution)/shard_map/reduce_sum | solution.py:66
  199.7 0.9 copy.24
  (37 shorter events, 0.3 us)
Async XLA Ops:
  19.5 7.4 %copy-start.5 = (bf16[256,768]{1,0:T(8,128)(2,1)S(1)}, bf16[256,768]{1,0:T(8,128)(2,1)}, u32[]{:S(2)}) copy-start(bf16[256,768]{1,0:T(8,128)(2,1)} %param.11) | copy-start | bytes 1179652
  19.5 44.5 %all-to-all-start.1 = ((bf16[16,64,768]{2,1,0:T(8,128)(2,1)}), bf16[16,64,768]{2,1,0:T(8,128)(2,1)S(1)}, u32[]{:S(2)}, u32[]{:S(2)}) async-start(bf16[16,64,768]{2,1,0:T(8,128)(2,1)} %bitcast.11), calls=%async_computation.1 | async-start | bytes 3145728 | tf_op jit(solution)/shard_map/all_to_all | solution.py:37
  26.8 4.0 %copy-start.7 = (f32[256,2]{0,1:T(2,128)S(1)}, f32[256,2]{0,1:T(2,128)}, u32[]{:S(2)}) copy-start(f32[256,2]{0,1:T(2,128)} %param.13) | copy-start | bytes 6148
  26.8 83.0 %all-gather.5.cloned.1.call-start = ((), (), s32[]{:S(2)}) async-start(), calls=%async_computation.6 | async-start | bytes 4718592 | tf_op jit(solution)/shard_map/all_gather | solution.py:41
  64.0 1.2 copy-start
  65.2 56.2 %all-gather.3.cloned.1.call-start = ((), (), s32[]{:S(2)}) async-start(), calls=%async_computation.5 | async-start | bytes 4718592 | tf_op jit(solution)/shard_map/all_gather | solution.py:42
  109.7 41.6 %reduce-scatter.3.cloned.1.call-start = ((), (), s32[]{:S(2)}) async-start(), calls=%async_computation.7 | async-start | bytes 4718592 | tf_op jit(solution)/shard_map/reduce_scatter | solution.py:58
  109.8 21.8 %slice-start = ((s8[4718592]{0:T(1024)(128)(4,1)}), s8[524288]{0:T(1024)(128)(4,1)S(1)}, s32[]{:S(2)}) async-start(s8[4718592]{0:T(1024)(128)(4,1)} %bitcast.107), calls=%async_computation.9 | async-start | bytes 1048576
  121.4 10.2 %slice-start.1 = ((s8[4718592]{0:T(1024)(128)(4,1)}), s8[4194304]{0:T(1024)(128)(4,1)S(1)}, s32[]{:S(2)}) async-start(s8[4718592]{0:T(1024)(128)(4,1)} %bitcast.107), calls=%async_computation.10 | async-start | bytes 8388608
  138.1 1.0 copy-start.3
  139.1 12.1 %collective-permute-start = (bf16[31,768]{1,0:T(8,128)(2,1)S(1)}, bf16[31,768]{1,0:T(8,128)(2,1)S(1)}, u32[]{:S(2)}, u32[]{:S(2)}) collective-permute-start(bf16[31,768]{1,0:T(8,128)(2,1)S(1)} %slice.210), channel_id=1, source_target_pairs={{2,0},{4,2},{6,4},{8,6},{10,8},{12,10},{14,12},{16,14},{18,16},{20... | collective-permute-start | bytes 142856 | tf_op jit(solution)/shard_map/ppermute | solution.py:10
  142.4 3.4 %copy-start.6 = (f32[32,768]{1,0:T(8,128)S(1)}, f32[32,768]{1,0:T(8,128)}, u32[]{:S(2)}) copy-start(f32[32,768]{1,0:T(8,128)} %param.18) | copy-start | bytes 294916
  142.5 3.5 %copy-start.4 = (bf16[256,768]{1,0:T(8,128)(2,1)S(1)}, bf16[256,768]{1,0:T(8,128)(2,1)}, u32[]{:S(2)}) copy-start(bf16[256,768]{1,0:T(8,128)(2,1)} %param.16) | copy-start | bytes 1179652
  145.8 5.3 %copy-start.1 = (bf16[192,8,2,768]{3,1,2,0:T(8,128)(2,1)}, bf16[192,8,2,768]{3,1,2,0:T(8,128)(2,1)S(1)}, u32[]{:S(2)}) copy-start(bf16[192,8,2,768]{3,1,2,0:T(8,128)(2,1)S(1)} %copy.27) | copy-start | bytes 14155780
  151.3 44.0 %all-to-all-start.2 = ((bf16[768,16,64]{0,2,1:T(8,128)(2,1)}), bf16[768,16,64]{0,2,1:T(8,128)(2,1)S(1)}, u32[]{:S(2)}, u32[]{:S(2)}) async-start(bf16[768,16,64]{0,2,1:T(8,128)(2,1)} %bitcast.103), calls=%async_computation.3 | async-start | bytes 3145728 | tf_op jit(solution)/shard_map/all_to_all | solution.py:64
  158.0 18.8 %reduce-scatter.5.cloned.1.call-start = ((), (), s32[]{:S(2)}) async-start(), calls=%async_computation.8 | async-start | bytes 1179648 | tf_op jit(solution)/shard_map/reduce_scatter | solution.py:80
  158.0 4.5 %copy-start.2 = (f32[256,1536]{1,0:T(8,128)S(1)}, f32[256,1536]{1,0:T(8,128)}, u32[]{:S(2)}) copy-start(f32[256,1536]{1,0:T(8,128)} %fusion.72) | copy-start | bytes 4718596
Sparse Core Ops, SparseCore 0:
  65.3 11.0 all-gather.4
  109.8 11.4 all-gather.2
  138.2 12.2 reduce-scatter.2
  167.5 9.2 reduce-scatter.4
where the time goes:
time: 208 us; the launch traced here: 207 us
  waiting for transfers between devices  60.7 us (29%)
  blocking collectives  42.8 us (21%)
  matrix products  33.6 us (16%)
  local copies, waits for them, and re-layouts  29.4 us (14%)
  starting transfers between devices  17.5 us (8%)
  between operations  14.1 us (7%)
  other arithmetic  9.01 us (4%)
    all_to_all x1, blocking collectives, body(): lax.all_to_all(g_send, 'expert', split_axis=0, concat_axis=0, tiled=True)  40.3 us
    all_to_all x1, waiting for transfers between devices, body(): lax.all_to_all(x_send, 'expert', split_axis=0, concat_axis=0, tiled=True)  32.9 us
    all_to_all x1, waiting for transfers between devices, body(): lax.all_to_all(slot_grads, 'expert', split_axis=1, concat_axis=1, tiled=T...  16.6 us
    dot_general x1, matrix products, body(): jnp.einsum('sqcd,qhd->sqch', g_part, w_out, preferred_element_type=jnp.fl...  10.2 us
    dot_general x1, matrix products, body(): jnp.einsum('sqcd,qdh->sqch', x_part, w_in, preferred_element_type=jnp.flo...  9.77 us
    reduce_scatter x1, waiting for transfers between devices, body(): lax.psum_scatter(lax.dot_general(rows_glu, glu_grad, (((1,), (1,)), ((),...  9.37 us
    unnamed x25, local copies, waits for them, and re-layouts  9.26 us
    all_to_all x1, starting transfers between devices, body(): lax.all_to_all(x_send, 'expert', split_axis=0, concat_axis=0, tiled=True)  7.3 us
  transfers between devices with their start and end apart: 7, of which 4 were waited for; matrix products, arithmetic and copies ran while one was open for 17% of the time, Pallas kernels for 0%

commit v1 on v0

--- a/solution.py
+++ b/solution.py
@@ -61,7 +61,12 @@
         scatter_dimension=0,
         tiled=True,
     )
-    returned = lax.all_to_all(slot_grads, "expert", split_axis=1, concat_axis=1, tiled=True)
+    returned = jnp.concatenate(
+        lax.all_to_all(
+            jnp.stack(jnp.split(slot_grads, lax.axis_size("expert"), axis=1)), "expert", 0, 0
+        ),
+        axis=1,
+    )
     picked = returned[:, slot].astype(jnp.float32).reshape(channels, frames, 2)
     moe_input_grad = jnp.sum(picked, axis=2).astype(jnp.bfloat16)
     taps = kernel.shape[0]

time: 208 us -> 233 us (1.12)
  local copies, waits for them, and re-layouts: 29.4 us -> 54 us
    unnamed x25 -> x40, local copies, waits for them, and re-layouts: 9.26 us -> 32.3 us
  transfers between devices with their start and end apart: 7 -> 7, of which waited for: 4 -> 4; matrix products, arithmetic and copies ran while one was open for 17% -> 15% of each run, Pallas kernels for 0% -> 0%
where the time goes in v1:
time: 233 us; the launch traced here: 232 us
  waiting for transfers between devices  60.7 us (26%)
  local copies, waits for them, and re-layouts  54 us (23%)
  blocking collectives  42.8 us (18%)
  matrix products  33.6 us (14%)
  starting transfers between devices  17.4 us (7%)
  between operations  14.1 us (6%)
  other arithmetic  9 us (4%)
    all_to_all x1, blocking collectives, body(): lax.all_to_all(g_send, 'expert', split_axis=0, concat_axis=0, tiled=True)  40.3 us
    all_to_all x1, waiting for transfers between devices, body(): lax.all_to_all(x_send, 'expert', split_axis=0, concat_axis=0, tiled=True)  32.9 us
    unnamed x40, local copies, waits for them, and re-layouts  32.3 us
    all_to_all x1, waiting for transfers between devices, body(): lax.all_to_all(jnp.stack(jnp.split(slot_grads, lax.axis_size('expert'), a...  16.6 us
    dot_general x1, matrix products, body(): jnp.einsum('sqcd,qhd->sqch', g_part, w_out, preferred_element_type=jnp.fl...  10.2 us
    dot_general x1, matrix products, body(): jnp.einsum('sqcd,qdh->sqch', x_part, w_in, preferred_element_type=jnp.flo...  9.77 us
    reduce_scatter x1, waiting for transfers between devices, body(): lax.psum_scatter(lax.dot_general(rows_glu, glu_grad, (((1,), (1,)), ((),...  9.37 us
    all_to_all x1, starting transfers between devices, body(): lax.all_to_all(x_send, 'expert', split_axis=0, concat_axis=0, tiled=True)  7.3 us
  transfers between devices with their start and end apart: 7, of which 4 were waited for; matrix products, arithmetic and copies ran while one was open for 15% of the time, Pallas kernels for 0%

profile of v1, /device:TPU:12, one launch (start us, length us, event | category | flops | bytes accessed | tf_op | source)
XLA Modules:
  0.0 231.7 jit_solution(12667137927302342387)
XLA Ops:
  7.2 0.8 copy.21
  8.3 0.7 broadcast_multiply_fusion
  9.0 1.1 reduce-window.6
  10.8 2.4 %scatter_custom_fusion = s32[1024]{0:T(1024)S(1)} fusion(s32[512]{0:T(512)S(1)} %bitcast.168, s32[512]{0:T(512)S(1)} %iota.11, s32[]{:T(128)} %constant.14.clone.1), kind=kCustom, calls=%fused_computation.185 | custom fusion | bytes 4100 | tf_op jit(solution)/shard_map/scatter | solution.py:28
  13.3 1.0 concatenate.14
  14.3 5.2 %gather_fusion.1 = bf16[1024,768]{1,0:T(8,128)(2,1)} fusion(bf16[257,768]{1,0:T(8,128)(2,1)S(1)} %concatenate.14, s32[1024]{0:T(1024)S(1)} %get-tuple-element.43), kind=kCustom, calls=%fused_computation.1 | custom fusion | bytes 3149824 | tf_op jit(solution)/shard_map/gather | solution.py:34
  19.5 7.3 %all-to-all-start.1 = ((bf16[16,64,768]{2,1,0:T(8,128)(2,1)}), bf16[16,64,768]{2,1,0:T(8,128)(2,1)S(1)}, u32[]{:S(2)}, u32[]{:S(2)}) async-start(bf16[16,64,768]{2,1,0:T(8,128)(2,1)} %bitcast.11), calls=%async_computation.1 | async-start | bytes 3145728 | tf_op jit(solution)/shard_map/all_to_all | solution.py:37
  26.9 1.6 mul.378
  28.4 2.4 %mul.379 = f32[512,768]{1,0:T(8,128)S(1)} reshape(f32[256,2,768]{2,1,0:T(2,128)} %mul.378) | data formatting | bytes 3145728 | tf_op jit(solution)/shard_map/mul | solution.py:29
  31.1 32.9 %all-to-all-done.1 = bf16[16,64,768]{2,1,0:T(8,128)(2,1)S(1)} async-done(((bf16[16,64,768]{2,1,0:T(8,128)(2,1)}), bf16[16,64,768]{2,1,0:T(8,128)(2,1)S(1)}, u32[]{:S(2)}, u32[]{:S(2)}) %all-to-all-start.1) | async-done | bytes 1572896 | tf_op jit(solution)/shard_map/all_to_all | solution.py:37
  64.0 1.2 copy-done
  65.4 4.0 %gather_fusion = bf16[1024,768]{1,0:T(8,128)(2,1)S(1)} fusion(bf16[513,768]{1,0:T(8,128)(2,1)S(1)} %concatenate.13, s32[1024]{0:T(1024)S(1)} %get-tuple-element.42), kind=kCustom, calls=%fused_computation | custom fusion | bytes 3149824 | tf_op jit(solution)/shard_map/gather | solution.py:35
  69.4 40.3 %all_to_all.29 = bf16[16,64,768]{2,1,0:T(8,128)(2,1)} all-to-all(bf16[16,64,768]{2,1,0:T(8,128)(2,1)S(1)} %bitcast.162), channel_id=1, replica_groups=mesh['expert'=16,'tensor'=2] {'expert'}, dimensions={0} | all-to-all | bytes 3145728 | tf_op jit(solution)/shard_map/all_to_all | solution.py:38
  109.8 9.8 %fusion.8 = f32[16,64,1536]{2,1,0:T(8,128)} fusion(bf16[16,64,1536]{2,1,0:T(8,128)(2,1)} %bitcast.173, bf16[1,1536,1536]{2,1,0:T(8,128)(2,1)} %param.14), kind=kOutput, calls=%fused_computation.15 | convolution fusion | flops 4831838208 | bytes 14155776 | tf_op jit(solution)/shard_map/sqcd,qdh->sqch/dot_general | solution.py:47
  119.6 1.8 all-gather.3.cloned.1.call-done
  121.4 10.2 %fusion.17 = bf16[16,64,1536]{2,1,0:T(8,128)(2,1)S(1)} fusion(f32[16,64,1536]{2,1,0:T(8,128)} %fusion.8, bf16[16,64,1536]{2,1,0:T(8,128)(2,1)} %bitcast.174, bf16[1,1536,1536]{2,1,0:T(8,128)(2,1)} %param.15), kind=kOutput, calls=%fused_computation.20 | convolution fusion | flops 4845993984 | bytes 17301504 | tf_op jit(solution)/shard_map/sqcd,qhd->sqch/dot_general | solution.py:48
  131.6 6.5 %fusion.14 = bf16[16,64,1536]{2,1,0:T(8,128)(2,1)} fusion(bf16[16,64,1536]{2,1,0:T(8,128)(2,1)S(1)} %fusion.17, bf16[1,1536,1536]{2,1,0:T(8,128)(2,1)S(1)} %bitcast.172), kind=kOutput, calls=%fused_computation.19 | convolution fusion | flops 4833411072 | bytes 11010048 | tf_op jit(solution)/shard_map/qih,sqch->isqc/dot_general | solution.py:57
  138.1 1.0 copy-done.3
  139.1 3.4 %collective-permute-start = (bf16[31,768]{1,0:T(8,128)(2,1)S(1)}, bf16[31,768]{1,0:T(8,128)(2,1)S(1)}, u32[]{:S(2)}, u32[]{:S(2)}) collective-permute-start(bf16[31,768]{1,0:T(8,128)(2,1)S(1)} %slice.210), channel_id=1, source_target_pairs={{2,0},{4,2},{6,4},{8,6},{10,8},{12,10},{14,12},{16,14},{18,16},{20... | collective-permute-start | bytes 142856 | tf_op jit(solution)/shard_map/ppermute | solution.py:10
  142.5 3.3 %copy.27 = bf16[192,8,2,768]{3,1,2,0:T(8,128)(2,1)S(1)} copy(bf16[192,8,2,768]{3,2,1,0:T(2,128)(2,1)} %bitcast.163) | data formatting | bytes 9437184
  146.0 2.5 %all_gather.11 = bf16[256,1536]{1,0:T(8,128)(2,1)S(1)} all-gather(bf16[256,768]{1,0:T(8,128)(2,1)S(1)} %copy-done.4), channel_id=1, replica_groups=mesh['expert'=16,'tensor'=2] {'tensor'}, dimensions={1}, use_global_device_ids=true | all-gather | bytes 1179648 | tf_op jit(solution)/shard_map/all_gather | solution.py:51
  148.5 2.6 %fusion.88 = f32[256,1536]{1,0:T(8,128)} fusion(bf16[256,1536]{1,0:T(8,128)(2,1)S(1)} %all_gather.11, bf16[1536,1536]{1,0:T(8,128)(2,1)S(1)} %bitcast.164), kind=kOutput, calls=%fused_computation.190 | convolution fusion | flops 1207959552 | bytes 7077888 | tf_op jit(solution)/shard_map/dot_general | solution.py:50
  151.3 1.5 fusion.76
  152.8 1.5 fusion.75
  154.4 1.5 fusion.74
  155.9 1.5 fusion.73
  157.4 1.5 fusion.72
  159.0 1.5 fusion.71
  160.5 1.5 fusion.70
  162.1 1.5 fusion.69
  163.6 1.5 fusion.68
  165.1 1.5 fusion.67
  166.7 1.5 fusion.66
  168.2 1.5 fusion.65
  169.7 1.5 fusion.64
  171.3 1.5 fusion.63
  172.8 1.5 fusion.62
  174.3 1.5 fusion.61
  175.9 6.6 %all-to-all-start.2 = ((bf16[16,768,64]{1,2,0:T(8,128)(2,1)}), bf16[16,768,64]{1,2,0:T(8,128)(2,1)S(1)}, u32[]{:S(2)}, u32[]{:S(2)}) async-start(bf16[16,768,64]{1,2,0:T(8,128)(2,1)} %fusion.61), calls=%async_computation.3 | async-start | bytes 3145728 | tf_op jit(solution)/shard_map/all_to_all | solution.py:65
  182.5 4.4 %multiply_convert_fusion.1 = (bf16[256,768]{1,0:T(8,128)(2,1)S(1)}, f32[256,768]{1,0:T(8,128)S(1)}) fusion(f32[256,1536]{1,0:T(8,128)} %fusion.88, f32[287,768]{1,0:T(8,128)S(1)} %maximum_convert_fusion, f32[768]{0:T(1024)S(1)} %get-tuple-element.38, f32[768]{0:T(1024)S(1)} %get-tuple-element.39, f32[768]{0:T(1024)S(1)} %get-tuple-element.9, ...), kind=kLoop, calls=%fused_computation.98 | loop fusion | flops 13369344 | bytes 27230208 | tf_op jit(solution)/shard_map/convert.1
  187.3 4.6 %fusion.20 = bf16[1536,256]{0,1:T(8,128)(2,1)} fusion(bf16[1536,1536]{1,0:T(8,128)(2,1)} %bitcast.165, bf16[256,768]{1,0:T(8,128)(2,1)S(1)} %fusion.23, bf16[256,768]{1,0:T(8,128)(2,1)S(1)} %get-tuple-element.40), kind=kOutput, calls=%fused_computation.22 | convolution fusion | flops 1209925632 | bytes 6291456 | tf_op jit(solution)/shard_map/dot_general | solution.py:86
  191.9 9.4 %reduce-scatter.5.cloned.1.call-done = bf16[768,256]{0,1:T(8,128)(2,1)} async-done(((bf16[1536,256]{0,1:T(8,128)(2,1)}), bf16[768,256]{0,1:T(8,128)(2,1)}) %reduce-scatter.5.cloned.1.call-update) | async-done | bytes 393232 | tf_op jit(solution)/shard_map/reduce_scatter | solution.py:85
  201.3 1.9 copy.25
  203.2 16.6 %all-to-all-done.2 = bf16[16,768,64]{1,2,0:T(8,128)(2,1)S(1)} async-done(((bf16[16,768,64]{1,2,0:T(8,128)(2,1)}), bf16[16,768,64]{1,2,0:T(8,128)(2,1)S(1)}, u32[]{:S(2)}, u32[]{:S(2)}) %all-to-all-start.2) | async-done | bytes 1572896 | tf_op jit(solution)/shard_map/all_to_all | solution.py:65
  219.8 2.0 gather_fusion.2
  221.8 0.3 gather.14
  222.1 2.1 reduce_sum.22
  224.2 0.9 copy.24
  (53 shorter events, 2.3 us)
Async XLA Ops:
  19.5 7.3 %copy-start.5 = (bf16[256,768]{1,0:T(8,128)(2,1)S(1)}, bf16[256,768]{1,0:T(8,128)(2,1)}, u32[]{:S(2)}) copy-start(bf16[256,768]{1,0:T(8,128)(2,1)} %param.11) | copy-start | bytes 1179652
  19.5 44.5 %all-to-all-start.1 = ((bf16[16,64,768]{2,1,0:T(8,128)(2,1)}), bf16[16,64,768]{2,1,0:T(8,128)(2,1)S(1)}, u32[]{:S(2)}, u32[]{:S(2)}) async-start(bf16[16,64,768]{2,1,0:T(8,128)(2,1)} %bitcast.11), calls=%async_computation.1 | async-start | bytes 3145728 | tf_op jit(solution)/shard_map/all_to_all | solution.py:37
  26.8 83.0 %all-gather.5.cloned.1.call-start = ((), (), s32[]{:S(2)}) async-start(), calls=%async_computation.6 | async-start | bytes 4718592 | tf_op jit(solution)/shard_map/all_gather | solution.py:41
  28.4 2.4 %copy-start.7 = (f32[256,2]{0,1:T(2,128)S(1)}, f32[256,2]{0,1:T(2,128)}, u32[]{:S(2)}) copy-start(f32[256,2]{0,1:T(2,128)} %param.13) | copy-start | bytes 6148
  64.0 1.2 copy-start
  65.1 56.2 %all-gather.3.cloned.1.call-start = ((), (), s32[]{:S(2)}) async-start(), calls=%async_computation.5 | async-start | bytes 4718592 | tf_op jit(solution)/shard_map/all_gather | solution.py:42
  109.7 41.6 %reduce-scatter.3.cloned.1.call-start = ((), (), s32[]{:S(2)}) async-start(), calls=%async_computation.7 | async-start | bytes 4718592 | tf_op jit(solution)/shard_map/reduce_scatter | solution.py:58
  109.8 21.8 %slice-start = ((s8[4718592]{0:T(1024)(128)(4,1)}), s8[524288]{0:T(1024)(128)(4,1)S(1)}, s32[]{:S(2)}) async-start(s8[4718592]{0:T(1024)(128)(4,1)} %bitcast.171), calls=%async_computation.9 | async-start | bytes 1048576
  121.4 10.2 %slice-start.1 = ((s8[4718592]{0:T(1024)(128)(4,1)}), s8[4194304]{0:T(1024)(128)(4,1)S(1)}, s32[]{:S(2)}) async-start(s8[4718592]{0:T(1024)(128)(4,1)} %bitcast.171), calls=%async_computation.10 | async-start | bytes 8388608
  138.1 1.0 copy-start.3
  139.1 12.1 %collective-permute-start = (bf16[31,768]{1,0:T(8,128)(2,1)S(1)}, bf16[31,768]{1,0:T(8,128)(2,1)S(1)}, u32[]{:S(2)}, u32[]{:S(2)}) collective-permute-start(bf16[31,768]{1,0:T(8,128)(2,1)S(1)} %slice.210), channel_id=1, source_target_pairs={{2,0},{4,2},{6,4},{8,6},{10,8},{12,10},{14,12},{16,14},{18,16},{20... | collective-permute-start | bytes 142856 | tf_op jit(solution)/shard_map/ppermute | solution.py:10
  142.4 3.4 %copy-start.6 = (f32[32,768]{1,0:T(8,128)S(1)}, f32[32,768]{1,0:T(8,128)}, u32[]{:S(2)}) copy-start(f32[32,768]{1,0:T(8,128)} %param.18) | copy-start | bytes 294916
  142.4 3.5 %copy-start.4 = (bf16[256,768]{1,0:T(8,128)(2,1)S(1)}, bf16[256,768]{1,0:T(8,128)(2,1)}, u32[]{:S(2)}) copy-start(bf16[256,768]{1,0:T(8,128)(2,1)} %param.16) | copy-start | bytes 1179652
  145.8 5.3 %copy-start.1 = (bf16[192,8,2,768]{3,1,2,0:T(8,128)(2,1)}, bf16[192,8,2,768]{3,1,2,0:T(8,128)(2,1)S(1)}, u32[]{:S(2)}) copy-start(bf16[192,8,2,768]{3,1,2,0:T(8,128)(2,1)S(1)} %copy.27) | copy-start | bytes 14155780
  175.9 43.9 %all-to-all-start.2 = ((bf16[16,768,64]{1,2,0:T(8,128)(2,1)}), bf16[16,768,64]{1,2,0:T(8,128)(2,1)S(1)}, u32[]{:S(2)}, u32[]{:S(2)}) async-start(bf16[16,768,64]{1,2,0:T(8,128)(2,1)} %fusion.61), calls=%async_computation.3 | async-start | bytes 3145728 | tf_op jit(solution)/shard_map/all_to_all | solution.py:65
  182.5 18.8 %reduce-scatter.5.cloned.1.call-start = ((), (), s32[]{:S(2)}) async-start(), calls=%async_computation.8 | async-start | bytes 1179648 | tf_op jit(solution)/shard_map/reduce_scatter | solution.py:85
  182.5 4.5 %copy-start.2 = (f32[256,1536]{1,0:T(8,128)S(1)}, f32[256,1536]{1,0:T(8,128)}, u32[]{:S(2)}) copy-start(f32[256,1536]{1,0:T(8,128)} %fusion.88) | copy-start | bytes 4718596
Sparse Core Ops, SparseCore 0:
  65.3 11.0 all-gather.4
  109.8 11.4 all-gather.2
  138.2 12.2 reduce-scatter.2
  192.0 9.2 reduce-scatter.4
